TPU v7x, 256 devices: a whole 4x4x8 slice. The times are simulated.
256 devices in a mesh: fsdp: 8 (over x_hi, y), ctx: 32 (over z, x_lo, core).
Axes of the slice: x: 4 (x_hi: 2, x_lo: 2; x = x_hi * 2 + x_lo), y: 4, z: 8, core: 2. Of those that a mesh axis runs over, the one named last changes fastest.
Arguments:
- tokens: bfloat16 [8, 4096, 1024], P('fsdp', 'ctx'), may hold values from -16 to 16
- cotangent: bfloat16 [8, 4096, 1024], P('fsdp', 'ctx'), may hold values from -6 to 6
- w_query: bfloat16 [1024, 512], P('fsdp')
- w_key: bfloat16 [1024, 512], P('fsdp')
- w_value: bfloat16 [1024, 512], P('fsdp'), may hold values from -0.1875 to 0.1875
- w_out: bfloat16 [512, 1024], P('fsdp'), may hold values from -0.25 to 0.25
- block_mask: int32 [32, 32], replicated, may hold values from 0 to 1, as said below
- span_order: int32 [64], replicated, may hold values from 0 to 63, each once
Outputs:
- mixed_out: bfloat16 [8, 4096, 1024], P('fsdp', 'ctx')
- token_grad: bfloat16 [8, 4096, 1024], P('fsdp', 'ctx')
- grad_query: float32 [1024, 512], P(('fsdp', 'ctx'))
- grad_key: float32 [1024, 512], P(('fsdp', 'ctx'))
- grad_value: float32 [1024, 512], P(('fsdp', 'ctx'))
- grad_out: float32 [512, 1024], P(('fsdp', 'ctx'))
Inputs may be any that keep to these rules, and one draw needn't show every extreme that they name: `block_mask`: every diagonal entry is 1.
All inputs are finite; a program needn't handle non-finite values.
Results may differ from a plain program's by a relative error of at most 0.013.
The roundings to bfloat16 on the way count: a program that leaves them out, or rounds other values in their place, can miss the bound.
Values may be sent and summed in bfloat16 or wider, within the bound.
No kernel may reach another device: no remote copies, remote signals or barrier semaphores. Data moves between devices by JAX's collectives and lax.ppermute only.
A program may use at most 128 MiB of HBM per device.

v0:
```python
import math
import jax
import jax.numpy as jnp
from jax import lax
from jax.sharding import PartitionSpec as P

HEADS = 4
HD = 128
BLK = 128
SPAN = 64
NEG = -1e30
HIGH = lax.Precision.HIGHEST


def block_ids(span_order, start, count):
    rows = start + jnp.arange(count, dtype=jnp.int32)
    span = rows // SPAN
    lanes = jnp.arange(span_order.shape[0], dtype=jnp.int32)
    first = jnp.sum(jnp.where(span[:, None] == lanes[None, :], span_order[None, :], 0), axis=1)
    return (first * SPAN + rows % SPAN) // BLK


def allowed_between(mask_f, row_ids, col_ids):
    lanes = jnp.arange(mask_f.shape[0], dtype=jnp.int32)
    left = (row_ids[:, None] == lanes[None, :]).astype(jnp.float32)
    right = (col_ids[:, None] == lanes[None, :]).astype(jnp.float32)
    linked = jnp.dot(jnp.dot(left, mask_f), right.T)
    return linked > 0.5


def over_blocks(step, carry, pieces):
    count = pieces[0].shape[0]
    width = 512
    stacked = tuple((piece.reshape((count // width, width) + piece.shape[1:]) for piece in pieces))

    def scan_step(state, item):
        number, parts = item
        return (step(state, parts, number * width), None)

    numbers = jnp.arange(count // width, dtype=jnp.int32)
    carry, _ = lax.scan(scan_step, carry, (numbers, stacked))
    return carry


def contract_rows(left, right):
    return lax.dot_general(
        left, right, (((0,), (0,)), ((), ())), preferred_element_type=jnp.float32
    )


def contract_cols(left, right):
    return lax.dot_general(
        left, right, (((1,), (1,)), ((), ())), preferred_element_type=jnp.float32
    )


def body(tokens, cotangent, w_query, w_key, w_value, w_out, block_mask, span_order):
    x_rows = tokens[0]
    dy_rows = cotangent[0]
    rows = x_rows.shape[0]
    scale = 1.0 / math.sqrt(HD)
    full_q, full_k, full_v, full_o = (
        lax.all_gather(w_query, "fsdp", axis=0, tiled=True),
        lax.all_gather(w_key, "fsdp", axis=0, tiled=True),
        lax.all_gather(w_value, "fsdp", axis=0, tiled=True),
        lax.all_gather(w_out, "fsdp", axis=0, tiled=True),
    )
    query = jnp.dot(x_rows, full_q, preferred_element_type=jnp.float32).astype(jnp.bfloat16)
    keys = jnp.dot(x_rows, full_k, preferred_element_type=jnp.float32).astype(jnp.bfloat16)
    values = jnp.dot(x_rows, full_v, preferred_element_type=jnp.float32).astype(jnp.bfloat16)
    d_attn = contract_cols(dy_rows, full_o).astype(jnp.bfloat16)
    mask_f = block_mask.astype(jnp.float32)
    own_ids = block_ids(span_order, lax.axis_index("ctx") * rows, rows)
    q_own = query.reshape(rows, HEADS, HD)
    k_own = keys.reshape(rows, HEADS, HD)
    v_own = values.reshape(rows, HEADS, HD)
    g_own = d_attn.reshape(rows, HEADS, HD)

    def sweep_keys(carry, parts, start):
        top, total, out_acc, mix_acc, key_acc, dot_acc = carry
        count = parts[0].shape[0]
        k_part = parts[0].reshape(count, HEADS, HD)
        v_part = parts[1].reshape(count, HEADS, HD)
        keep = allowed_between(mask_f, own_ids, block_ids(span_order, start, count))[None]
        score = (
            jnp.einsum("qhd,khd->hqk", q_own, k_part, preferred_element_type=jnp.float32) * scale
        )
        score = jnp.where(keep, score, NEG)
        new_top = jnp.maximum(top, jnp.max(score, axis=-1))
        fade = jnp.exp(top - new_top)
        prob = jnp.where(keep, jnp.exp(score - new_top[:, :, None]), 0.0)
        k_wide = k_part.astype(jnp.float32)
        v_wide = v_part.astype(jnp.float32)
        total = fade * total + jnp.sum(prob, axis=-1)
        out_acc = fade[:, :, None] * out_acc + jnp.einsum(
            "hqk,khd->hqd", prob, v_wide, precision=HIGH
        )
        d_prob = jnp.einsum("qhd,khd->hqk", g_own, v_part, preferred_element_type=jnp.float32)
        weighted = prob * d_prob
        dot_acc = fade * dot_acc + jnp.sum(weighted, axis=-1)
        mix_acc = fade[:, :, None] * mix_acc + jnp.einsum(
            "hqk,khd->hqd", weighted, k_wide, precision=HIGH
        )
        key_acc = fade[:, :, None] * key_acc + jnp.einsum(
            "hqk,khd->hqd", prob, k_wide, precision=HIGH
        )
        return (new_top, total, out_acc, mix_acc, key_acc, dot_acc)

    flat = jnp.zeros((HEADS, rows), jnp.float32)
    cube = jnp.zeros((HEADS, rows, HD), jnp.float32)
    begin = (jnp.full((HEADS, rows), NEG, jnp.float32), flat, cube, cube, cube, flat)
    top, total, out_acc, mix_acc, key_acc, dot_acc = over_blocks(
        sweep_keys,
        begin,
        (
            lax.all_gather(keys, "ctx", axis=0, tiled=True),
            lax.all_gather(values, "ctx", axis=0, tiled=True),
        ),
    )
    share = 1.0 / total
    combined = out_acc * share[:, :, None]
    log_total = top + jnp.log(total)
    attention = jnp.transpose(combined, (1, 0, 2)).reshape(rows, HEADS * HD).astype(jnp.bfloat16)
    mixed = (
        x_rows.astype(jnp.float32) + jnp.dot(attention, full_o, preferred_element_type=jnp.float32)
    ).astype(jnp.bfloat16)
    delta = dot_acc * share
    log_rows = jnp.transpose(log_total)
    delta_rows = jnp.transpose(delta)

    def key_side(acc, parts, start):
        d_key, d_value = acc
        count = parts[0].shape[0]
        q_part = parts[0].reshape(count, HEADS, HD)
        g_part = parts[1].reshape(count, HEADS, HD)
        lse_part = jnp.transpose(parts[2])
        delta_part = jnp.transpose(parts[3])
        keep = allowed_between(mask_f, block_ids(span_order, start, count), own_ids)[None]
        score = (
            jnp.einsum("khd,qhd->hkq", q_part, k_own, preferred_element_type=jnp.float32) * scale
        )
        score = jnp.where(keep, score, NEG)
        prob = jnp.where(keep, jnp.exp(score - lse_part[:, :, None]), 0.0)
        d_prob = jnp.einsum("khd,qhd->hkq", g_part, v_own, preferred_element_type=jnp.float32)
        d_score = prob * (d_prob - delta_part[:, :, None])
        d_key = d_key + scale * jnp.einsum(
            "hkq,khd->hqd", d_score, q_part.astype(jnp.float32), precision=HIGH
        )
        d_value = d_value + jnp.einsum(
            "hkq,khd->hqd", prob, g_part.astype(jnp.float32), precision=HIGH
        )
        return (d_key, d_value)

    d_query = scale * (mix_acc - delta[:, :, None] * key_acc) * share[:, :, None]
    d_key, d_value = over_blocks(
        key_side,
        (cube, cube),
        (
            lax.all_gather(query.astype(jnp.float32), "ctx", axis=0, tiled=True).astype(
                jnp.bfloat16
            ),
            lax.all_gather(d_attn.astype(jnp.float32), "ctx", axis=0, tiled=True).astype(
                jnp.bfloat16
            ),
            lax.all_gather(log_rows, "ctx", axis=0, tiled=True),
            lax.all_gather(delta_rows, "ctx", axis=0, tiled=True),
        ),
    )

    def to_rows(grad_heads):
        return jnp.transpose(grad_heads, (1, 0, 2)).reshape(rows, HEADS * HD).astype(jnp.bfloat16)

    dq_rows = to_rows(d_query)
    dk_rows = to_rows(d_key)
    dv_rows = to_rows(d_value)
    token_grad = (
        dy_rows.astype(jnp.float32)
        + contract_cols(dq_rows, full_q)
        + contract_cols(dk_rows, full_k)
        + contract_cols(dv_rows, full_v)
    ).astype(jnp.bfloat16)
    grad_q = contract_rows(x_rows, dq_rows)
    grad_k = contract_rows(x_rows, dk_rows)
    grad_v = contract_rows(x_rows, dv_rows)
    grad_o = contract_rows(attention, dy_rows)
    grad_q, grad_k, grad_v, grad_o = (
        lax.psum_scatter(grad_q, ("fsdp", "ctx"), scatter_dimension=0, tiled=True),
        lax.psum_scatter(grad_k, ("fsdp", "ctx"), scatter_dimension=0, tiled=True),
        lax.psum_scatter(grad_v, ("fsdp", "ctx"), scatter_dimension=0, tiled=True),
        lax.psum_scatter(grad_o, ("fsdp", "ctx"), scatter_dimension=0, tiled=True),
    )
    return (mixed[None], token_grad[None], grad_q, grad_k, grad_v, grad_o)


def solution(mesh):
    return jax.shard_map(
        body,
        mesh=mesh,
        in_specs=(
            P("fsdp", "ctx", None),
            P("fsdp", "ctx", None),
            P("fsdp", None),
            P("fsdp", None),
            P("fsdp", None),
            P("fsdp", None),
            P(),
            P(),
        ),
        out_specs=(
            P("fsdp", "ctx", None),
            P("fsdp", "ctx", None),
            P(("fsdp", "ctx"), None),
            P(("fsdp", "ctx"), None),
            P(("fsdp", "ctx"), None),
            P(("fsdp", "ctx"), None),
        ),
        check_vma=False,
    )
```

profile of v0, /device:TPU:2, one launch (start us, length us, event | category | flops | bytes accessed | tf_op | source)
XLA Modules:
  0.0 907.5 jit_solution(11538158528910636079)
XLA Ops:
  10.0 54.1 %all-gather.9.cloned.1.call-done = bf16[1024,512]{1,0:T(8,128)(2,1)} async-done(((bf16[128,512]{1,0:T(8,128)(2,1)}), bf16[1024,512]{1,0:T(8,128)(2,1)}) %all-gather.9.cloned.1.call-update) | async-done | bytes 1048592 | tf_op jit(solution)/shard_map/all_gather | solution.py:64
  66.5 50.6 %all-gather.15.cloned.1.call-done = bf16[1024,512]{1,0:T(8,128)(2,1)} async-done(((bf16[128,512]{1,0:T(8,128)(2,1)}), bf16[1024,512]{1,0:T(8,128)(2,1)}) %all-gather.15.cloned.1.call-update) | async-done | bytes 1048592 | tf_op jit(solution)/shard_map/all_gather | solution.py:65
  119.3 50.7 %all-gather.13.cloned.1.call-done = bf16[1024,512]{1,0:T(8,128)(2,1)} async-done(((bf16[128,512]{1,0:T(8,128)(2,1)}), bf16[1024,512]{1,0:T(8,128)(2,1)}) %all-gather.13.cloned.1.call-update) | async-done | bytes 1048592 | tf_op jit(solution)/shard_map/all_gather | solution.py:63
  175.9 46.9 %all-gather.19.cloned.1.call-done = bf16[512,1024]{1,0:T(8,128)(2,1)} async-done(((bf16[64,1024]{1,0:T(8,128)(2,1)}), bf16[512,1024]{1,0:T(8,128)(2,1)}) %all-gather.19.cloned.1.call-update) | async-done | bytes 1048592 | tf_op jit(solution)/shard_map/all_gather | solution.py:66
  225.2 65.8 %all-gather.11.cloned.1.call-done = bf16[4096,512]{1,0:T(8,128)(2,1)} async-done(((bf16[128,512]{1,0:T(8,128)(2,1)}), bf16[4096,512]{1,0:T(8,128)(2,1)}) %all-gather.11.cloned.1.call-update) | async-done | bytes 4194320 | tf_op jit(solution)/shard_map/all_gather | solution.py:116
  291.1 68.8 %all-gather.17.cloned.1.call-done = bf16[4096,512]{1,0:T(8,128)(2,1)} async-done(((bf16[128,512]{1,0:T(8,128)(2,1)}), bf16[4096,512]{1,0:T(8,128)(2,1)}) %all-gather.17.cloned.1.call-update) | async-done | bytes 4194320 | tf_op jit(solution)/shard_map/all_gather | solution.py:117
  360.4 75.2 %while.40 = (s32[]{:T(128)}, f32[4,128]{1,0:T(4,128)S(1)}, f32[4,128]{1,0:T(4,128)S(1)}, f32[4,128,128]{2,1,0:T(8,128)S(1)}, f32[4,128,128]{2,1,0:T(8,128)S(1)},...) while((s32[]{:T(128)}, f32[4,128]{1,0:T(4,128)S(1)}, ...), condition=%wide.region_6.7_spmd.clone, body=%wide.region_1.6_spmd.clone.sunk | while | flops 1351104000 | bytes 16581600 | solution.py:41
  438.1 34.6 %all_gather.37 = f32[4096,4]{0,1:T(4,128)} all-gather(f32[128,4]{0,1:T(4,128)S(1)} %get-tuple-element.758), channel_id=1, replica_groups=mesh['fsdp'=8,'ctx'=32] {'ctx'}, dimensions={0}, use_global_device_ids=true | all-gather | bytes 67584 | tf_op jit(solution)/shard_map/all_gather | solution.py:165
  472.7 33.9 %all_gather.39 = f32[4096,4]{0,1:T(4,128)} all-gather(f32[128,4]{0,1:T(4,128)S(1)} %bitcast.204), channel_id=1, replica_groups=mesh['fsdp'=8,'ctx'=32] {'ctx'}, dimensions={0}, use_global_device_ids=true | all-gather | bytes 67584 | tf_op jit(solution)/shard_map/all_gather | solution.py:166
  507.2 97.2 %while.41 = (s32[]{:T(128)}, f32[4,128,128]{2,1,0:T(8,128)}, f32[4,128,128]{2,1,0:T(8,128)}, s32[8]{0:T(128)}, s32[64]{0:T(128)S(1)}, /*index=5*/bf16[32,32]{1,0...) while((s32[]{:T(128)}, f32[4,128,128]{2,1,0:T(8,128)}, ...), condition=%wide.region_9.10_spmd.clone, body=%wide.region_7.9_spmd.clone.sunk | while | flops 946874368 | bytes 14089224 | solution.py:41
  524.6 2.7 fusion.146
  527.4 2.7 convolution_add_fusion.15
  537.0 2.7 fusion.146
  539.8 2.7 convolution_add_fusion.15
  549.4 2.7 fusion.146
  552.1 2.7 convolution_add_fusion.15
  561.8 2.7 fusion.146
  564.5 2.6 convolution_add_fusion.15
  574.2 2.7 fusion.146
  576.9 2.7 convolution_add_fusion.15
  586.5 2.7 fusion.146
  589.3 2.7 convolution_add_fusion.15
  598.9 2.7 fusion.146
  621.2 273.0 %all-reduce.7.cloned.1.call-done = (f32[1024,512]{0,1:T(8,128)}, f32[1024,512]{0,1:T(8,128)}, f32[1024,512]{0,1:T(8,128)}, f32[512,1024]{1,0:T(8,128)}) async-done(((f32[1024,512]{0,1:T(8,128)}, f32[1024,512]{0,1:T(8,128)}, f32[1024,512]{0,1:T(8,128)}, f32[512,1024]{1,0:T(8,128)}), (f32[1024,512]{0,1:T(8,128)}, f32[1024,512]{0,1:T(8,128)}, f32[1024,512]{0,1:T(8,128)}, ...) | async-done | bytes 8388624
  (376 shorter events, 168.4 us)
Async XLA Ops:
  7.2 109.9 %copy-start = (bf16[1,128,1024]{2,1,0:T(8,128)(2,1)S(1)}, bf16[1,128,1024]{2,1,0:T(8,128)(2,1)}, u32[]{:S(2)}) copy-start(bf16[1,128,1024]{2,1,0:T(8,128)(2,1)} %param.12) | copy-start | bytes 786436
  7.2 56.9 %all-gather.9.cloned.1.call-start = ((), (), s32[]{:S(2)}) async-start(), calls=%async_computation | async-start | bytes 1179648 | tf_op jit(solution)/shard_map/all_gather | solution.py:64
  7.9 109.1 %all-gather.15.cloned.1.call-start = ((), (), s32[]{:S(2)}) async-start(), calls=%async_computation.3 | async-start | bytes 1179648 | tf_op jit(solution)/shard_map/all_gather | solution.py:65
  8.7 161.3 %all-gather.13.cloned.1.call-start = ((), (), s32[]{:S(2)}) async-start(), calls=%async_computation.2 | async-start | bytes 1179648 | tf_op jit(solution)/shard_map/all_gather | solution.py:63
  9.4 213.4 %all-gather.19.cloned.1.call-start = ((), (), s32[]{:S(2)}) async-start(), calls=%async_computation.5 | async-start | bytes 1179648 | tf_op jit(solution)/shard_map/all_gather | solution.py:66
  10.0 162.4 %copy-start.19 = (s32[32,32]{1,0:T(8,128)S(1)}, s32[32,32]{1,0:T(8,128)}, u32[]{:S(2)}) copy-start(s32[32,32]{1,0:T(8,128)} %param.18) | copy-start | bytes 12292
  10.0 163.0 %copy-start.16 = (s32[64]{0:T(128)S(1)}, s32[64]{0:T(128)}, u32[]{:S(2)}) copy-start(s32[64]{0:T(128)} %param.19) | copy-start | bytes 772
  10.0 281.1 %all-gather.11.cloned.1.call-start = ((), (), s32[]{:S(2)}) async-start(), calls=%async_computation.1 | async-start | bytes 4325376 | tf_op jit(solution)/shard_map/all_gather | solution.py:116
  66.4 108.1 %copy-start.9 = (bf16[128,512]{1,0:T(8,128)(2,1)S(1)}, bf16[128,512]{1,0:T(8,128)(2,1)}, u32[]{:S(2)}) copy-start(bf16[128,512]{1,0:T(8,128)(2,1)} %convolution_convert_fusion.3) | copy-start | bytes 393220
  66.4 156.4 %copy-start.6 = (bf16[1,128,1024]{2,1,0:T(8,128)(2,1)S(1)}, bf16[1,128,1024]{2,1,0:T(8,128)(2,1)}, u32[]{:S(2)}) copy-start(bf16[1,128,1024]{2,1,0:T(8,128)(2,1)} %param.13) | copy-start | bytes 786436
  66.4 293.4 %all-gather.17.cloned.1.call-start = ((), (), s32[]{:S(2)}) async-start(), calls=%async_computation.4 | async-start | bytes 4325376 | tf_op jit(solution)/shard_map/all_gather | solution.py:117
  119.2 56.0 %copy-start.10 = (bf16[128,512]{1,0:T(8,128)(2,1)S(1)}, bf16[128,512]{1,0:T(8,128)(2,1)}, u32[]{:S(2)}) copy-start(bf16[128,512]{1,0:T(8,128)(2,1)} %convolution_convert_fusion.1) | copy-start | bytes 393220
  119.3 387.3 %all-gather.21.cloned.1.call-start = ((), (), s32[]{:S(2)}) async-start(), calls=%async_computation.6 | async-start | bytes 4325376 | tf_op jit(solution)/shard_map/all_gather | solution.py:159
  172.2 334.4 %all-gather.23.cloned.1.call-start = ((), (), s32[]{:S(2)}) async-start(), calls=%async_computation.7 | async-start | bytes 4325376 | tf_op jit(solution)/shard_map/all_gather | solution.py:162
  225.2 669.0 %all-reduce.7.cloned.1.call-start = ((), (), s32[]{:S(2)}) async-start(), calls=%async_computation.8 | async-start | bytes 16777216
  438.1 69.1 %copy-start.17 = (f32[4,128]{1,0:T(4,128)}, f32[4,128]{1,0:T(4,128)S(1)}, u32[]{:S(2)}) copy-start(f32[4,128]{1,0:T(4,128)S(1)} %get-tuple-element.746) | copy-start | bytes 6148
  438.1 69.1 %copy-start.18 = (f32[4,128]{1,0:T(4,128)}, f32[4,128]{1,0:T(4,128)S(1)}, u32[]{:S(2)}) copy-start(f32[4,128]{1,0:T(4,128)S(1)} %get-tuple-element.747) | copy-start | bytes 6148
  507.2 5.5 copy-start.15
  517.6 5.5 copy-start.15
  530.0 5.5 copy-start.15
  542.4 5.5 copy-start.15
  554.8 5.5 copy-start.15
  567.2 5.5 copy-start.15
  579.5 5.5 copy-start.15
  (19 other events, 76.5 us)
Sparse Core Ops, SparseCore 0:
  10.7 53.4 all-gather.8
  66.8 50.2 all-gather.14
  119.7 50.2 all-gather.12
  172.5 50.2 all-gather.18
  225.0 65.9 all-gather.10
  293.4 66.4 all-gather.16
  361.7 66.6 all-gather.20
  430.3 66.8 all-gather.22
  614.9 279.2 all-reduce.6
where the time goes:
time: 910 us; the launch traced here: 908 us
  waiting for transfers between devices  612 us (67%)
  matrix products  122 us (13%)
  local copies, waits for them, and re-layouts  71.7 us (8%)
  blocking collectives  68.5 us (8%)
  between operations  14.1 us (2%)
  loops' own time  11.7 us (1%)
    unnamed x10, waiting for transfers between devices  276 us
    all_gather x1, waiting for transfers between devices, body(): lax.all_gather(values, 'ctx', axis=0, tiled=True)  68.8 us
    all_gather x1, waiting for transfers between devices, body(): lax.all_gather(keys, 'ctx', axis=0, tiled=True)  65.8 us
    all_gather x1, waiting for transfers between devices, body(): lax.all_gather(w_key, 'fsdp', axis=0, tiled=True)  54.1 us
    all_gather x1, waiting for transfers between devices, body(): lax.all_gather(w_query, 'fsdp', axis=0, tiled=True)  50.7 us
    all_gather x1, waiting for transfers between devices, body(): lax.all_gather(w_value, 'fsdp', axis=0, tiled=True)  50.6 us
    dynamic_slice x64, local copies, waits for them, and re-layouts, over_blocks(): carry, _ = lax.scan(scan_step, carry, (numbers, stacked))  47.6 us
    all_gather x1, waiting for transfers between devices, body(): lax.all_gather(w_out, 'fsdp', axis=0, tiled=True)  46.9 us
  transfers between devices with their start and end apart: 9, of which 7 were waited for; matrix products, arithmetic and copies ran while one was open for 10% of the time, Pallas kernels for 0%

commit v1 on v0

--- a/solution.py
+++ b/solution.py
@@ -114,7 +114,9 @@
         begin,
         (
             lax.all_gather(keys, "ctx", axis=0, tiled=True),
-            lax.all_gather(values, "ctx", axis=0, tiled=True),
+            jnp.concatenate(
+                lax.all_to_all(jnp.stack([values] * lax.axis_size("ctx")), "ctx", 0, 0), axis=0
+            ),
         ),
     )
     share = 1.0 / total

time: 910 us -> 865 us (0.951)
  waiting for transfers between devices: 612 us -> 557 us
    all_gather x1 -> x0, waiting for transfers between devices: 68.8 us -> none  [body(): lax.all_gather(values, 'ctx', axis=0, tiled=True)]
    all_gather x1, waiting for transfers between devices: 65.8 us -> 79.6 us  [body(): lax.all_gather(keys, 'ctx', axis=0, tiled=True)]
    unnamed x10 -> x9, waiting for transfers between devices: 276 us -> 275 us
  transfers between devices with their start and end apart: 9 -> 9, of which waited for: 7 -> 6; matrix products, arithmetic and copies ran while one was open for 10% -> 11% of each run, Pallas kernels for 0% -> 0%
where the time goes in v1:
time: 865 us; the launch traced here: 863 us
  waiting for transfers between devices  557 us (64%)
  matrix products  122 us (14%)
  local copies, waits for them, and re-layouts  74 us (9%)
  blocking collectives  67.3 us (8%)
  between operations  14.4 us (2%)
  loops' own time  12.1 us (1%)
  starting transfers between devices  9.15 us (1%)
    unnamed x9, waiting for transfers between devices  275 us
    all_gather x1, waiting for transfers between devices, body(): lax.all_gather(keys, 'ctx', axis=0, tiled=True)  79.6 us
    all_gather x1, waiting for transfers between devices, body(): lax.all_gather(w_key, 'fsdp', axis=0, tiled=True)  54.1 us
    all_gather x1, waiting for transfers between devices, body(): lax.all_gather(w_value, 'fsdp', axis=0, tiled=True)  50.7 us
    all_gather x1, waiting for transfers between devices, body(): lax.all_gather(w_query, 'fsdp', axis=0, tiled=True)  50.6 us
    dynamic_slice x64, local copies, waits for them, and re-layouts, over_blocks(): carry, _ = lax.scan(scan_step, carry, (numbers, stacked))  48 us
    all_gather x1, waiting for transfers between devices, body(): lax.all_gather(w_out, 'fsdp', axis=0, tiled=True)  46.5 us
    all_gather x1, blocking collectives, body(): lax.all_gather(delta_rows, 'ctx', axis=0, tiled=True)  33.8 us
  transfers between devices with their start and end apart: 9, of which 6 were waited for; matrix products, arithmetic and copies ran while one was open for 11% of the time, Pallas kernels for 0%

profile of v1, /device:TPU:2, one launch (start us, length us, event | category | flops | bytes accessed | tf_op | source)
XLA Modules:
  0.0 862.6 jit_solution(12292728135193235116)
XLA Ops:
  10.0 54.1 %all-gather.8.cloned.1.call-done = bf16[1024,512]{1,0:T(8,128)(2,1)} async-done(((bf16[128,512]{1,0:T(8,128)(2,1)}), bf16[1024,512]{1,0:T(8,128)(2,1)}) %all-gather.8.cloned.1.call-update) | async-done | bytes 1048592 | tf_op jit(solution)/shard_map/all_gather | solution.py:64
  66.5 50.6 %all-gather.12.cloned.1.call-done = bf16[1024,512]{1,0:T(8,128)(2,1)} async-done(((bf16[128,512]{1,0:T(8,128)(2,1)}), bf16[1024,512]{1,0:T(8,128)(2,1)}) %all-gather.12.cloned.1.call-update) | async-done | bytes 1048592 | tf_op jit(solution)/shard_map/all_gather | solution.py:63
  119.3 50.7 %all-gather.14.cloned.1.call-done = bf16[1024,512]{1,0:T(8,128)(2,1)} async-done(((bf16[128,512]{1,0:T(8,128)(2,1)}), bf16[1024,512]{1,0:T(8,128)(2,1)}) %all-gather.14.cloned.1.call-update) | async-done | bytes 1048592 | tf_op jit(solution)/shard_map/all_gather | solution.py:65
  174.0 8.8 %all-to-all-start = ((bf16[32,128,512]{2,1,0:T(8,128)(2,1)}), bf16[32,128,512]{2,1,0:T(8,128)(2,1)}, u32[]{:S(2)}, u32[]{:S(2)}) async-start(bf16[32,128,512]{2,1,0:T(8,128)(2,1)} %stack.2), calls=%async_computation | async-start | bytes 8388608 | tf_op jit(solution)/shard_map/all_to_all | solution.py:118
  184.2 46.5 %all-gather.16.cloned.1.call-done = bf16[512,1024]{1,0:T(8,128)(2,1)} async-done(((bf16[64,1024]{1,0:T(8,128)(2,1)}), bf16[512,1024]{1,0:T(8,128)(2,1)}) %all-gather.16.cloned.1.call-update) | async-done | bytes 1048592 | tf_op jit(solution)/shard_map/all_gather | solution.py:66
  235.5 79.6 %all-gather.10.cloned.1.call-done = bf16[4096,512]{1,0:T(8,128)(2,1)} async-done(((bf16[128,512]{1,0:T(8,128)(2,1)}), bf16[4096,512]{1,0:T(8,128)(2,1)}) %all-gather.10.cloned.1.call-update) | async-done | bytes 4194320 | tf_op jit(solution)/shard_map/all_gather | solution.py:116
  315.6 75.2 %while.40 = (s32[]{:T(128)}, f32[4,128]{1,0:T(4,128)S(1)}, f32[4,128]{1,0:T(4,128)S(1)}, f32[4,128,128]{2,1,0:T(8,128)S(1)}, f32[4,128,128]{2,1,0:T(8,128)S(1)},...) while((s32[]{:T(128)}, f32[4,128]{1,0:T(4,128)S(1)}, ...), condition=%wide.region_6.7_spmd.clone, body=%wide.region_1.6_spmd.clone.sunk | while | flops 1351104000 | bytes 16581600 | solution.py:41
  393.3 33.5 %all_gather.33 = f32[4096,4]{0,1:T(4,128)} all-gather(f32[128,4]{0,1:T(4,128)S(1)} %get-tuple-element.792), channel_id=1, replica_groups=mesh['fsdp'=8,'ctx'=32] {'ctx'}, dimensions={0}, use_global_device_ids=true | all-gather | bytes 67584 | tf_op jit(solution)/shard_map/all_gather | solution.py:167
  426.8 33.8 %all_gather.35 = f32[4096,4]{0,1:T(4,128)} all-gather(f32[128,4]{0,1:T(4,128)S(1)} %bitcast.203), channel_id=1, replica_groups=mesh['fsdp'=8,'ctx'=32] {'ctx'}, dimensions={0}, use_global_device_ids=true | all-gather | bytes 67584 | tf_op jit(solution)/shard_map/all_gather | solution.py:168
  461.2 98.1 %while.41 = (s32[]{:T(128)}, f32[4,128,128]{2,1,0:T(8,128)}, f32[4,128,128]{2,1,0:T(8,128)}, s32[8]{0:T(128)}, s32[64]{0:T(128)S(1)}, /*index=5*/bf16[32,32]{1,0...) while((s32[]{:T(128)}, f32[4,128,128]{2,1,0:T(8,128)}, ...), condition=%wide.region_9.10_spmd.clone, body=%wide.region_7.9_spmd.clone.sunk | while | flops 946874368 | bytes 14089224 | solution.py:41
  478.9 2.7 fusion.146
  481.6 2.7 convolution_add_fusion.15
  491.4 2.7 fusion.146
  494.1 2.7 convolution_add_fusion.15
  503.9 2.7 fusion.146
  506.6 2.7 convolution_add_fusion.15
  516.4 2.7 fusion.146
  519.1 2.7 convolution_add_fusion.15
  528.9 2.7 fusion.146
  531.6 2.7 convolution_add_fusion.15
  541.4 2.7 fusion.146
  544.1 2.7 convolution_add_fusion.15
  553.9 2.7 fusion.146
  576.2 272.8 %all-reduce.7.cloned.1.call-done = (f32[1024,512]{0,1:T(8,128)}, f32[1024,512]{0,1:T(8,128)}, f32[1024,512]{0,1:T(8,128)}, f32[512,1024]{1,0:T(8,128)}) async-done(((f32[1024,512]{0,1:T(8,128)}, f32[1024,512]{0,1:T(8,128)}, f32[1024,512]{0,1:T(8,128)}, f32[512,1024]{1,0:T(8,128)}), (f32[1024,512]{0,1:T(8,128)}, f32[1024,512]{0,1:T(8,128)}, f32[1024,512]{0,1:T(8,128)}, ...) | async-done | bytes 8388624
  (374 shorter events, 170.6 us)
Async XLA Ops:
  7.2 109.9 %copy-start = (bf16[1,128,1024]{2,1,0:T(8,128)(2,1)S(1)}, bf16[1,128,1024]{2,1,0:T(8,128)(2,1)}, u32[]{:S(2)}) copy-start(bf16[1,128,1024]{2,1,0:T(8,128)(2,1)} %param.12) | copy-start | bytes 786436
  7.2 56.9 %all-gather.8.cloned.1.call-start = ((), (), s32[]{:S(2)}) async-start(), calls=%async_computation.1 | async-start | bytes 1179648 | tf_op jit(solution)/shard_map/all_gather | solution.py:64
  7.9 109.1 %all-gather.12.cloned.1.call-start = ((), (), s32[]{:S(2)}) async-start(), calls=%async_computation.3 | async-start | bytes 1179648 | tf_op jit(solution)/shard_map/all_gather | solution.py:63
  8.7 161.3 %all-gather.14.cloned.1.call-start = ((), (), s32[]{:S(2)}) async-start(), calls=%async_computation.4 | async-start | bytes 1179648 | tf_op jit(solution)/shard_map/all_gather | solution.py:65
  9.4 221.3 %all-gather.16.cloned.1.call-start = ((), (), s32[]{:S(2)}) async-start(), calls=%async_computation.5 | async-start | bytes 1179648 | tf_op jit(solution)/shard_map/all_gather | solution.py:66
  10.0 305.1 %all-gather.10.cloned.1.call-start = ((), (), s32[]{:S(2)}) async-start(), calls=%async_computation.2 | async-start | bytes 4325376 | tf_op jit(solution)/shard_map/all_gather | solution.py:116
  66.4 394.2 %all-gather.18.cloned.1.call-start = ((), (), s32[]{:S(2)}) async-start(), calls=%async_computation.6 | async-start | bytes 4325376 | tf_op jit(solution)/shard_map/all_gather | solution.py:161
  174.0 9.0 %copy-start.18 = (s32[32,32]{1,0:T(8,128)S(1)}, s32[32,32]{1,0:T(8,128)}, u32[]{:S(2)}) copy-start(s32[32,32]{1,0:T(8,128)} %param.18) | copy-start | bytes 12292
  174.0 9.6 %copy-start.15 = (s32[64]{0:T(128)S(1)}, s32[64]{0:T(128)}, u32[]{:S(2)}) copy-start(s32[64]{0:T(128)} %param.19) | copy-start | bytes 772
  174.0 56.7 %copy-start.6 = (bf16[1,128,1024]{2,1,0:T(8,128)(2,1)S(1)}, bf16[1,128,1024]{2,1,0:T(8,128)(2,1)}, u32[]{:S(2)}) copy-start(bf16[1,128,1024]{2,1,0:T(8,128)(2,1)} %param.13) | copy-start | bytes 786436
  174.0 59.2 %copy-start.8 = (bf16[128,512]{1,0:T(8,128)(2,1)S(1)}, bf16[128,512]{1,0:T(8,128)(2,1)}, u32[]{:S(2)}) copy-start(bf16[128,512]{1,0:T(8,128)(2,1)} %convolution_convert_fusion.2) | copy-start | bytes 393220
  174.0 141.1 %all-to-all-start = ((bf16[32,128,512]{2,1,0:T(8,128)(2,1)}), bf16[32,128,512]{2,1,0:T(8,128)(2,1)}, u32[]{:S(2)}, u32[]{:S(2)}) async-start(bf16[32,128,512]{2,1,0:T(8,128)(2,1)} %stack.2), calls=%async_computation | async-start | bytes 8388608 | tf_op jit(solution)/shard_map/all_to_all | solution.py:118
  182.8 51.3 %copy-start.9 = (bf16[128,512]{1,0:T(8,128)(2,1)S(1)}, bf16[128,512]{1,0:T(8,128)(2,1)}, u32[]{:S(2)}) copy-start(bf16[128,512]{1,0:T(8,128)(2,1)} %convolution_convert_fusion.3) | copy-start | bytes 393220
  182.8 277.8 %all-gather.20.cloned.1.call-start = ((), (), s32[]{:S(2)}) async-start(), calls=%async_computation.7 | async-start | bytes 4325376 | tf_op jit(solution)/shard_map/all_gather | solution.py:164
  233.1 615.9 %all-reduce.7.cloned.1.call-start = ((), (), s32[]{:S(2)}) async-start(), calls=%async_computation.8 | async-start | bytes 16777216
  393.3 67.9 %copy-start.16 = (f32[4,128]{1,0:T(4,128)}, f32[4,128]{1,0:T(4,128)S(1)}, u32[]{:S(2)}) copy-start(f32[4,128]{1,0:T(4,128)S(1)} %get-tuple-element.780) | copy-start | bytes 6148
  393.3 67.9 %copy-start.17 = (f32[4,128]{1,0:T(4,128)}, f32[4,128]{1,0:T(4,128)S(1)}, u32[]{:S(2)}) copy-start(f32[4,128]{1,0:T(4,128)S(1)} %get-tuple-element.781) | copy-start | bytes 6148
  461.2 5.6 copy-start.14
  471.8 5.6 copy-start.14
  484.3 5.6 copy-start.14
  509.3 5.6 copy-start.14
  521.8 5.6 copy-start.14
  534.3 5.6 copy-start.14
  546.8 5.6 copy-start.14
  (18 other events, 76.9 us)
Sparse Core Ops, SparseCore 0:
  10.7 53.4 all-gather.7
  66.8 50.2 all-gather.11
  119.7 50.2 all-gather.13
  172.5 58.1 all-gather.15
  233.0 82.0 all-gather.9
  316.8 64.7 all-gather.17
  383.4 66.4 all-gather.19
  569.9 279.0 all-reduce.6
